TPU v7x, 32 devices: a whole 2x2x4 slice. The times are simulated.
32 devices in a mesh: row: 2 (over y), pair: 16 (over z, x, core).
Axes of the slice: x: 2, y: 2, z: 4, core: 2. Of those that a mesh axis runs over, the one named last changes fastest.
Arguments:
- panel: float32 [4096, 4096], P('row', 'pair'), may hold values from -51 to 51
- slot_block: int32 [32], replicated, may hold values from 0 to 31, each once
Outputs:
- rotated: float32 [4096, 4096], P('row', 'pair')
Inputs may be any that keep to these rules, and one draw needn't show every extreme that they name: `slot_block`: each block number appears once.
All inputs are finite; a program needn't handle non-finite values.
Results may differ from a plain program's by a relative error of at most 0.0003.
Values sent between devices are 32-bit elements; how exact they have to be, the bound alone decides.
A program may use at most 64 MiB of HBM per device.

v0:
```python
import jax
import jax.numpy as jnp
from jax import lax
from jax.sharding import PartitionSpec as P

STEPS = 2
NS_ITERS = 3


precise = lax.Precision.HIGHEST


def passed_along(value, axis, steps):
    count = lax.axis_size(axis)
    initial, last = (max(0, -steps), min(count, count - steps))
    return lax.ppermute(value, axis, [(source, source + steps) for source in range(initial, last)])


def inverse_root(matrix):
    identity = jnp.eye(matrix.shape[0], dtype=matrix.dtype)
    approx = matrix
    root_inv = identity
    for sweep in range(NS_ITERS):
        factor = 1.5 * identity - 0.5 * jnp.dot(root_inv, approx, precision=precise)
        approx = jnp.dot(approx, factor, precision=precise)
        root_inv = jnp.dot(factor, root_inv, precision=precise)
    return root_inv / jnp.sqrt(5.0)


def couple(cross):
    identity = jnp.eye(cross.shape[0], dtype=cross.dtype)
    coupling = cross * (2.0 / jnp.sqrt(jnp.sum(cross * cross) + 1e-06))
    left = (identity + jnp.dot(coupling, coupling.T, precision=precise)) / 5.0
    right = (identity + jnp.dot(coupling.T, coupling, precision=precise)) / 5.0
    return (coupling, left, right)


def inner_rows(first, second):
    return lax.dot_general(first, second, (((0,), (0,)), ((), ())), precision=precise)


def move_slots(uppers, lowers):
    new_uppers = jnp.concatenate([uppers[0:1], lowers[0:1], uppers[1:-1]], axis=0)
    new_lowers = jnp.concatenate([lowers[1:], uppers[-1:]], axis=0)
    return (new_uppers, new_lowers)


def jacobi_step(upper, lower, upper_ids, lower_ids, position, pairs):
    matching = jnp.arange(pairs) == position
    upper_id = jnp.sum(jnp.where(matching, upper_ids, 0))
    lower_id = jnp.sum(jnp.where(matching, lower_ids, 0))
    order_flag = upper_id < lower_id
    first = jnp.where(order_flag, upper, lower)
    second = jnp.where(order_flag, lower, upper)
    cross = lax.psum(inner_rows(first, second), "row")
    coupling, left, right = couple(cross)
    left_inverse = inverse_root(left)
    right_inverse = inverse_root(right)
    new_first = jnp.dot(
        first + jnp.dot(second, coupling.T, precision=precise), left_inverse, precision=precise
    )
    new_second = jnp.dot(
        second - jnp.dot(first, coupling, precision=precise), right_inverse, precision=precise
    )
    new_upper = jnp.where(order_flag, new_first, new_second)
    new_lower = jnp.where(order_flag, new_second, new_first)
    carried = jnp.where(position == 0, new_lower, new_upper)
    from_left = passed_along(carried, "pair", 1)
    from_right = passed_along(new_lower, "pair", -1)
    moved_upper = jnp.where(position == 0, new_upper, from_left)
    moved_lower = jnp.where(position == pairs - 1, new_upper, from_right)
    return (moved_upper, moved_lower)


def per_device(panel, slot_block):
    width = panel.shape[1] // 2
    pairs = lax.axis_size("pair")
    position = lax.axis_index("pair")
    upper = panel[:, :width]
    lower = panel[:, width:]
    upper_ids = slot_block[:pairs]
    lower_ids = slot_block[pairs:]
    for step in range(STEPS):
        upper, lower = jacobi_step(upper, lower, upper_ids, lower_ids, position, pairs)
        upper_ids, lower_ids = move_slots(upper_ids, lower_ids)
    return jnp.concatenate([upper, lower], axis=1)


def solution(mesh):
    in_specs = (P("row", "pair"), P())
    out_specs = P("row", "pair")
    return jax.shard_map(
        per_device, mesh=mesh, in_specs=in_specs, out_specs=out_specs, check_vma=False
    )
```

profile of v0, /device:TPU:1, one launch (start us, length us, event | category | flops | bytes accessed | tf_op | source)
XLA Modules:
  0.0 149.6 jit_solution(13770389145376605013)
XLA Ops:
  6.5 1.5 %select_reduce_fusion = (s32[]{:T(128)}, s32[]{:T(128)}) fusion(s32[32]{0:T(128)} %param.3, s32[]{:T(128)S(6)} %axis_index.12), kind=kLoop, calls=%fused_computation.82 | loop fusion | flops 78 | bytes 140 | tf_op jit(solution)/shard_map/reduce_sum | solution.py:51
  9.4 1.7 %slice_select_fusion.1 = (f32[2048,128]{1,0:T(8,128)S(1)}, f32[2048,128]{1,0:T(8,128)S(1)}) fusion(f32[2048,256]{1,0:T(8,128)} %param.2, pred[]{:T(512)S(6)} %lt.7), kind=kLoop, calls=%fused_computation.42 | loop fusion | flops 524288 | bytes 4194305 | tf_op jit(solution)/shard_map/jit(_where)/select_n | solution.py:53
  11.1 2.4 %fusion.39 = f32[128,128]{1,0:T(8,128)} fusion(f32[2048,128]{1,0:T(8,128)S(1)} %get-tuple-element.15, f32[2048,128]{1,0:T(8,128)S(1)} %get-tuple-element.16), kind=kOutput, calls=%fused_computation.86 | convolution fusion | flops 402653184 | bytes 2162688 | tf_op jit(solution)/shard_map/dot_general | solution.py:39
  13.6 22.7 %all-reduce.3.cloned.1.call-done = f32[128,128]{1,0:T(8,128)} async-done(((f32[128,128]{1,0:T(8,128)}), f32[128,128]{1,0:T(8,128)}) %all-reduce.3.cloned.1.call-update) | async-done | bytes 65552 | tf_op jit(solution)/shard_map/psum | solution.py:55
  36.3 1.5 %multiply_reduce_fusion.1 = f32[]{:T(128)} fusion(f32[128,128]{1,0:T(8,128)} %all-reduce.3.cloned.1.call-done), kind=kLoop, calls=%fused_computation.61 | loop fusion | flops 32767 | bytes 65540 | tf_op jit(solution)/shard_map/reduce_sum | solution.py:32
  38.5 1.2 fusion.11
  39.9 0.2 fusion.44
  40.3 0.2 fusion.9
  40.9 1.2 fusion.15
  42.7 0.2 fusion.13
  42.9 0.2 fusion.41
  43.1 0.2 fusion.42
  43.4 0.2 fusion.8
  43.6 0.2 convolution_multiply_fusion.8
  43.8 0.2 fusion.12
  44.0 0.2 convolution_multiply_fusion.12
  44.2 1.0 convolution_add_fusion.1
  45.2 1.0 fusion.43
  46.2 1.0 convolution_subtract_fusion.1
  47.2 2.0 %broadcast_select_fusion.11 = (f32[2048,128]{1,0:T(8,128)}, f32[2048,128]{1,0:T(8,128)S(1)}, f32[2048,128]{1,0:T(8,128)S(1)}) fusion(pred[]{:T(512)S(6)} %eq.72, f32[2048,128]{1,0:T(8,128)S(1)} %fusion.43, pred[]{:T(512)S(6)} %lt.7, f32[2048,128]{1,0:T(8,128)S(1)} %convolution_subtract_fusion.1, f32[128,128]{1,0:T(8,128)S(1)} %convolution_multiply_fusion.8), kind=kOutput, calls=%fused_computation.54 | convolution fusion | flops 403439616 | bytes 5308418 | tf_op jit(solution)/shard_map/dot_general | solution.py:62
  49.2 4.1 %collective-permute-start = (f32[2048,128]{1,0:T(8,128)}, f32[2048,128]{1,0:T(8,128)S(1)}, u32[]{:S(2)}, u32[]{:S(2)}) collective-permute-start(f32[2048,128]{1,0:T(8,128)} %get-tuple-element.10), channel_id=1, source_target_pairs={{0,1},{1,2},{2,3},{3,4},{4,5},{5,6},{6,7},{7,8},{8,9},{9,10},{10,1... | collective-permute-start | bytes 3145736 | tf_op jit(solution)/shard_map/ppermute | solution.py:16
  53.3 2.1 %collective-permute-start.1 = (f32[2048,128]{1,0:T(8,128)S(1)}, f32[2048,128]{1,0:T(8,128)}, u32[]{:S(2)}, u32[]{:S(2)}) collective-permute-start(f32[2048,128]{1,0:T(8,128)S(1)} %get-tuple-element.11), channel_id=1, source_target_pairs={{1,0},{2,1},{3,2},{4,3},{5,4},{6,5},{7,6},{8,7},{9,8},{10,9},{11,1... | collective-permute-start | bytes 3145736 | tf_op jit(solution)/shard_map/ppermute | solution.py:16
  55.6 0.7 fusion.38
  56.2 2.6 %fusion.36 = (s32[]{:T(128)}, s32[]{:T(128)}) fusion(s32[14]{0:T(128)S(1)} %slice.34, s32[1]{0:T(128)} %get-tuple-element.20, s32[1]{0:T(128)} %get-tuple-element.21, s32[]{:T(128)S(6)} %axis_index.12, s32[1]{0:T(128)} %get-tuple-element.19, s32[15]{0:T(128)S(1)} %slice.35), kind=kLoop, calls=%fused_computation.79 | loop fusion | flops 126 | bytes 140 | tf_op jit(solution)/shard_map/reduce_sum | solution.py:50
  60.1 16.5 %collective-permute-done = f32[2048,128]{1,0:T(8,128)S(1)} collective-permute-done((f32[2048,128]{1,0:T(8,128)}, f32[2048,128]{1,0:T(8,128)S(1)}, u32[]{:S(2)}, u32[]{:S(2)}) %collective-permute-start) | collective-permute-done | bytes 1048608 | tf_op jit(solution)/shard_map/ppermute | solution.py:16
  76.6 1.0 copy-done.2
  77.5 1.7 %broadcast_select_fusion.7 = (f32[2048,128]{1,0:T(8,128)S(1)}, f32[2048,128]{1,0:T(8,128)S(1)}) fusion(pred[]{:T(512)S(6)} %lt.6, f32[2048,128]{1,0:T(8,128)S(1)} %get-tuple-element.12, f32[2048,128]{1,0:T(8,128)} %copy-done.2, pred[]{:T(512)S(6)} %eq.72, f32[2048,128]{1,0:T(8,128)} %collective-permute-done.1, pred[]{:T(512)S(6)} %eq.76), kind=kLoop, calls=%fused_computation.50 | loop fusion | flops 1048576 | bytes 5242883 | tf_op jit(solution)/shard_map/jit(_where)/select_n | solution.py:53
  79.3 2.4 %fusion.47 = f32[128,128]{1,0:T(8,128)} fusion(f32[2048,128]{1,0:T(8,128)S(1)} %get-tuple-element.13, f32[2048,128]{1,0:T(8,128)S(1)} %get-tuple-element.14), kind=kOutput, calls=%fused_computation.94 | convolution fusion | flops 402653184 | bytes 2162688 | tf_op jit(solution)/shard_map/dot_general | solution.py:39
  81.7 20.4 %all-reduce.5.cloned.1.call-done = f32[128,128]{1,0:T(8,128)} async-done(((f32[128,128]{1,0:T(8,128)}), f32[128,128]{1,0:T(8,128)}) %all-reduce.5.cloned.1.call-update) | async-done | bytes 65552 | tf_op jit(solution)/shard_map/psum | solution.py:55
  102.1 1.5 %multiply_reduce_fusion = f32[]{:T(128)} fusion(f32[128,128]{1,0:T(8,128)} %all-reduce.5.cloned.1.call-done), kind=kLoop, calls=%fused_computation.55 | loop fusion | flops 32767 | bytes 65540 | tf_op jit(solution)/shard_map/reduce_sum | solution.py:32
  104.3 1.2 fusion.3
  105.7 0.2 fusion.52
  106.1 0.2 fusion.1
  106.7 1.2 fusion.7
  108.5 0.2 fusion.5
  108.7 0.2 fusion.49
  108.9 0.2 fusion.50
  109.2 0.2 fusion
  109.6 0.2 fusion.4
  109.8 0.2 convolution_multiply_fusion.4
  110.0 1.0 convolution_add_fusion
  111.0 1.0 fusion.51
  112.0 1.0 convolution_subtract_fusion
  113.0 1.0 broadcast_select_fusion.9
  114.0 4.1 %collective-permute-start.2 = (f32[2048,128]{1,0:T(8,128)S(1)}, f32[2048,128]{1,0:T(8,128)S(1)}, u32[]{:S(2)}, u32[]{:S(2)}) collective-permute-start(f32[2048,128]{1,0:T(8,128)S(1)} %get-tuple-element.7), channel_id=1, source_target_pairs={{0,1},{1,2},{2,3},{3,4},{4,5},{5,6},{6,7},{7,8},{8,9},{9,10},{10,1... | collective-permute-start | bytes 3145736 | tf_op jit(solution)/shard_map/ppermute | solution.py:16
  118.1 1.9 %collective-permute-start.3 = (f32[2048,128]{1,0:T(8,128)S(1)}, f32[2048,128]{1,0:T(8,128)S(1)}, u32[]{:S(2)}, u32[]{:S(2)}) collective-permute-start(f32[2048,128]{1,0:T(8,128)S(1)} %get-tuple-element.8), channel_id=1, source_target_pairs={{1,0},{2,1},{3,2},{4,3},{5,4},{6,5},{7,6},{8,7},{9,8},{10,9},{11,1... | collective-permute-start | bytes 3145736 | tf_op jit(solution)/shard_map/ppermute | solution.py:16
  120.1 21.0 %collective-permute-done.2 = f32[2048,128]{1,0:T(8,128)S(1)} collective-permute-done((f32[2048,128]{1,0:T(8,128)S(1)}, f32[2048,128]{1,0:T(8,128)S(1)}, u32[]{:S(2)}, u32[]{:S(2)}) %collective-permute-start.2) | collective-permute-done | bytes 1048608 | tf_op jit(solution)/shard_map/ppermute | solution.py:16
  141.3 1.5 pad_maximum_fusion
  (31 shorter events, 3.3 us)
Async XLA Ops:
  6.5 29.7 %all-reduce.3.cloned.1.call-start = ((), (), s32[]{:S(2)}) async-start(), calls=%async_computation | async-start | bytes 131072 | tf_op jit(solution)/shard_map/psum | solution.py:55
  13.6 88.5 %all-reduce.5.cloned.1.call-start = ((), (), s32[]{:S(2)}) async-start(), calls=%async_computation.1 | async-start | bytes 131072 | tf_op jit(solution)/shard_map/psum | solution.py:55
  36.3 7.9 %copy-start = (f32[128,128]{1,0:T(8,128)S(1)}, f32[128,128]{1,0:T(8,128)}, u32[]{:S(2)}) copy-start(f32[128,128]{1,0:T(8,128)} %all-reduce.3.cloned.1.call-done) | copy-start | bytes 196612
  47.2 8.2 %copy-start.3 = (s32[32]{0:T(128)S(1)}, s32[32]{0:T(128)}, u32[]{:S(2)}) copy-start(s32[32]{0:T(128)} %param.3) | copy-start | bytes 388
  49.2 27.4 %collective-permute-start = (f32[2048,128]{1,0:T(8,128)}, f32[2048,128]{1,0:T(8,128)S(1)}, u32[]{:S(2)}, u32[]{:S(2)}) collective-permute-start(f32[2048,128]{1,0:T(8,128)} %get-tuple-element.10), channel_id=1, source_target_pairs={{0,1},{1,2},{2,3},{3,4},{4,5},{5,6},{6,7},{7,8},{8,9},{9,10},{10,1... | collective-permute-start | bytes 3145736 | tf_op jit(solution)/shard_map/ppermute | solution.py:16
  53.3 23.3 %collective-permute-start.1 = (f32[2048,128]{1,0:T(8,128)S(1)}, f32[2048,128]{1,0:T(8,128)}, u32[]{:S(2)}, u32[]{:S(2)}) collective-permute-start(f32[2048,128]{1,0:T(8,128)S(1)} %get-tuple-element.11), channel_id=1, source_target_pairs={{1,0},{2,1},{3,2},{4,3},{5,4},{6,5},{7,6},{8,7},{9,8},{10,9},{11,1... | collective-permute-start | bytes 3145736 | tf_op jit(solution)/shard_map/ppermute | solution.py:16
  76.6 1.0 copy-start.2
  102.1 7.9 %copy-start.1 = (f32[128,128]{1,0:T(8,128)S(1)}, f32[128,128]{1,0:T(8,128)}, u32[]{:S(2)}) copy-start(f32[128,128]{1,0:T(8,128)} %all-reduce.5.cloned.1.call-done) | copy-start | bytes 196612
  114.0 27.1 %collective-permute-start.2 = (f32[2048,128]{1,0:T(8,128)S(1)}, f32[2048,128]{1,0:T(8,128)S(1)}, u32[]{:S(2)}, u32[]{:S(2)}) collective-permute-start(f32[2048,128]{1,0:T(8,128)S(1)} %get-tuple-element.7), channel_id=1, source_target_pairs={{0,1},{1,2},{2,3},{3,4},{4,5},{5,6},{6,7},{7,8},{8,9},{9,10},{10,1... | collective-permute-start | bytes 3145736 | tf_op jit(solution)/shard_map/ppermute | solution.py:16
  118.1 23.0 %collective-permute-start.3 = (f32[2048,128]{1,0:T(8,128)S(1)}, f32[2048,128]{1,0:T(8,128)S(1)}, u32[]{:S(2)}, u32[]{:S(2)}) collective-permute-start(f32[2048,128]{1,0:T(8,128)S(1)} %get-tuple-element.8), channel_id=1, source_target_pairs={{1,0},{2,1},{3,2},{4,3},{5,4},{6,5},{7,6},{8,7},{9,8},{10,9},{11,1... | collective-permute-start | bytes 3145736 | tf_op jit(solution)/shard_map/ppermute | solution.py:16
Sparse Core Ops, SparseCore 0:
  13.7 22.5 all-reduce.2
  81.9 20.1 all-reduce.4
where the time goes:
time: 151 us; the launch traced here: 150 us
  waiting for transfers between devices  80.6 us (53%)
  matrix products  24.9 us (16%)
  between operations  17.7 us (12%)
  starting transfers between devices  12.3 us (8%)
  other arithmetic  12.3 us (8%)
  local copies, waits for them, and re-layouts  1.79 us (1%)
    psum x2, waiting for transfers between devices, jacobi_step(): cross = lax.psum(inner_rows(first, second), 'row')  43 us
    ppermute x4, waiting for transfers between devices, passed_along(): lax.ppermute(value, axis, [(source, source + steps) for source in range(i...  37.5 us
    ppermute x4, starting transfers between devices, passed_along(): lax.ppermute(value, axis, [(source, source + steps) for source in range(i...  12.2 us
    dot_general x2, matrix products, inner_rows(): lax.dot_general(first, second, (((0,), (0,)), ((), ())), precision=precise)  4.89 us
    select_n x2, other arithmetic, jacobi_step(): first = jnp.where(order_flag, upper, lower)  3.4 us
    reduce_sum x2, other arithmetic, couple(): coupling = cross * (2.0 / jnp.sqrt(jnp.sum(cross * cross) + 1e-06))  3.06 us
  transfers between devices with their start and end apart: 6, of which 4 were waited for; matrix products, arithmetic and copies ran while one was open for 2% of the time, Pallas kernels for 0%

commit v1 on v0

v1 whole, which is shorter than its diff:
```python
import functools
import math

import jax
import jax.numpy as jnp
from jax import lax
from jax.experimental import pallas as pl
from jax.experimental.pallas import tpu as pltpu
from jax.sharding import PartitionSpec as P

STEPS = 2
NS_ITERS = 3
CHUNKS = 8
MESH = pl.DeviceIdType.MESH
F32 = jnp.float32
BF16 = jnp.bfloat16


def split(value):
    high = value.astype(BF16)
    return high, (value - high.astype(F32)).astype(BF16)


def raw_dot(a, b):
    return jnp.dot(a, b, preferred_element_type=F32)


def product(a, b):
    (a_high, a_low), (b_high, b_low) = a, b
    return raw_dot(a_high, b_high) + (raw_dot(a_high, b_low) + raw_dot(a_low, b_high))


def inner_rows(upper, lower):
    width = upper.shape[1]
    both = lax.dot_general(
        jnp.concatenate(split(upper), axis=1),
        jnp.concatenate(split(lower), axis=1),
        (((0,), (0,)), ((), ())),
        preferred_element_type=F32,
    )
    small = both[:width, width:] + both[width:, :width] + both[width:, width:]
    return both[:width, :width] + small


def identity_of(size):
    rows = lax.broadcasted_iota(jnp.int32, (size, size), 0)
    columns = lax.broadcasted_iota(jnp.int32, (size, size), 1)
    return jnp.where(rows == columns, 1.0, 0.0).astype(F32)


def inverse_root(matrix, identity):
    factor = 1.5 * identity - 0.5 * matrix
    root_inv = factor
    approx = matrix
    for sweep in range(1, NS_ITERS):
        factor_parts = split(factor)
        approx = product(split(approx), factor_parts)
        root_parts = split(root_inv)
        factor = 1.5 * identity - 0.5 * product(root_parts, split(approx))
        root_inv = product(split(factor), root_parts)
    return root_inv * (1.0 / math.sqrt(5.0))


def rotation(cross, sign):
    identity = identity_of(cross.shape[0])
    coupling = cross * (sign * (2.0 * lax.rsqrt(jnp.sum(cross * cross, keepdims=True) + 1e-06)))
    turned = coupling.T
    coupling_parts, turned_parts = split(coupling), split(turned)
    left = (identity + product(coupling_parts, turned_parts)) * 0.2
    right = (identity + product(turned_parts, coupling_parts)) * 0.2
    left_inverse = inverse_root(left, identity)
    right_inverse = inverse_root(right, identity)
    from_lower = product(turned_parts, split(left_inverse))
    from_upper = -product(coupling_parts, split(right_inverse))
    return jnp.concatenate(
        [
            jnp.concatenate([left_inverse, from_upper], axis=1),
            jnp.concatenate([from_lower, right_inverse], axis=1),
        ],
        axis=0,
    )


def kernel(
    rows_axis, pairs, ids, panel, out,
    start, uppers, lowers, to_right, to_left, weights, crosses,
    load_sem, cross_send, cross_recv, right_send, right_recv, left_send, left_recv, keep_sem,
):
    width = panel.shape[1] // 2
    chunk = panel.shape[0] // CHUNKS
    position = lax.axis_index("pair")
    row = lax.axis_index("row")
    first, last = position == 0, position == pairs - 1
    right, left = lax.rem(position + 1, pairs), lax.rem(position + pairs - 1, pairs)

    def load(index):
        return pltpu.make_async_copy(
            panel.at[pl.ds(index * chunk, chunk), :], start.at[index], load_sem.at[index]
        )

    def start_load(index, carry):
        load(index).start()
        return carry

    lax.fori_loop(0, CHUNKS, start_load, 0)

    barrier = pltpu.get_barrier_semaphore()
    for offset in range(1, rows_axis):
        peer = lax.rem(row + offset, rows_axis)
        pl.semaphore_signal(barrier, inc=1, device_id={"row": peer}, device_id_type=MESH)

    @pl.when(jnp.logical_not(first))
    def _():
        pl.semaphore_signal(barrier, inc=1, device_id={"pair": left}, device_id_type=MESH)

    @pl.when(jnp.logical_not(last))
    def _():
        pl.semaphore_signal(barrier, inc=1, device_id={"pair": right}, device_id_type=MESH)

    def sign_of(upper_id, lower_id):
        return jnp.where(upper_id < lower_id, 1.0, -1.0).astype(F32)

    moved_upper = jnp.where(first, ids[0], jnp.where(position == 1, ids[pairs], ids[left]))
    moved_lower = jnp.where(last, ids[pairs - 1], ids[pairs + right])
    signs = (
        sign_of(ids[position], ids[pairs + position]),
        sign_of(moved_upper, moved_lower),
    )

    def send_right(step, index):
        if step == 0:
            target = uppers.at[index]
        else:
            target = out.at[pl.ds(index * chunk, chunk), pl.ds(0, width)]
        return pltpu.make_async_remote_copy(
            src_ref=to_right.at[step, index],
            dst_ref=target,
            send_sem=right_send.at[step, index],
            recv_sem=right_recv.at[step, index],
            device_id={"pair": right},
            device_id_type=MESH,
        )

    def send_left(step, index):
        if step == 0:
            target = lowers.at[index]
        else:
            target = out.at[pl.ds(index * chunk, chunk), pl.ds(width, width)]
        return pltpu.make_async_remote_copy(
            src_ref=to_left.at[step, index],
            dst_ref=target,
            send_sem=left_send.at[step, index],
            recv_sem=left_recv.at[step, index],
            device_id={"pair": left},
            device_id_type=MESH,
        )

    def keep_upper(index):
        return pltpu.make_async_copy(
            uppers.at[index],
            out.at[pl.ds(index * chunk, chunk), pl.ds(0, width)],
            keep_sem.at[index],
        )

    def keep_lower(index):
        return pltpu.make_async_copy(
            lowers.at[index],
            out.at[pl.ds(index * chunk, chunk), pl.ds(width, width)],
            keep_sem.at[index],
        )

    def exchange(step, offset):
        peer = lax.rem(row + offset, rows_axis)
        return pltpu.make_async_remote_copy(
            src_ref=crosses.at[step, row],
            dst_ref=crosses.at[step, row],
            send_sem=cross_send.at[step, offset - 1],
            recv_sem=cross_recv.at[step, offset - 1],
            device_id={"row": peer},
            device_id_type=MESH,
        )

    for step in range(STEPS):

        def halves(index):
            if step == 0:
                return start[index, :, :width], start[index, :, width:]
            return uppers[index], lowers[index]

        def add_chunk(index, total):
            if step == 0:
                load(index).wait()
            else:

                @pl.when(jnp.logical_not(first))
                def _():
                    send_right(0, index).wait_recv()

                @pl.when(jnp.logical_not(last))
                def _():
                    send_left(0, index).wait_recv()

            return total + inner_rows(*halves(index))

        total = lax.fori_loop(0, CHUNKS, add_chunk, jnp.zeros((width, width), F32))
        crosses[step, row] = total
        if step == 0:
            neighbours = jnp.where(first, 0, 1) + jnp.where(last, 0, 1)
            pl.semaphore_wait(barrier, rows_axis - 1 + neighbours)
        copies = [exchange(step, offset) for offset in range(1, rows_axis)]
        for copy in copies:
            copy.start()
        for copy in copies:
            copy.wait()
        cross = crosses[step, 0]
        for index in range(1, rows_axis):
            cross = cross + crosses[step, index]
        for part, value in enumerate(split(rotation(cross, signs[step]))):
            weights[part] = value

        def turn_chunk(index, carry):
            upper, lower = halves(index)
            parts = split(jnp.concatenate([upper, lower], axis=1))
            turned = product(parts, (weights[0], weights[1]))
            new_upper, new_lower = turned[:, :width], turned[:, width:]
            to_right[step, index] = jnp.where(first, new_lower, new_upper)
            to_left[step, index] = new_lower

            @pl.when(jnp.logical_not(last))
            def _():
                send_right(step, index).start()

            @pl.when(jnp.logical_not(first))
            def _():
                send_left(step, index).start()

            @pl.when(first)
            def _():
                uppers[index] = new_upper
                if step == STEPS - 1:
                    keep_upper(index).start()

            @pl.when(last)
            def _():
                lowers[index] = new_upper
                if step == STEPS - 1:
                    keep_lower(index).start()

            return carry

        lax.fori_loop(0, CHUNKS, turn_chunk, 0)

    def finish(index, carry):
        @pl.when(jnp.logical_not(last))
        def _():
            send_right(0, index).wait_send()
            send_right(1, index).wait_send()
            send_left(1, index).wait_recv()

        @pl.when(jnp.logical_not(first))
        def _():
            send_left(0, index).wait_send()
            send_left(1, index).wait_send()
            send_right(1, index).wait_recv()

        @pl.when(first)
        def _():
            keep_upper(index).wait()

        @pl.when(last)
        def _():
            keep_lower(index).wait()

        return carry

    lax.fori_loop(0, CHUNKS, finish, 0)


def solution(mesh):
    rows_axis, pairs = mesh.shape["row"], mesh.shape["pair"]

    def per_device(panel, slot_block):
        rows, width = panel.shape[0], panel.shape[1] // 2
        chunk = rows // CHUNKS
        dma = pltpu.SemaphoreType.DMA
        return pl.pallas_call(
            functools.partial(kernel, rows_axis, pairs),
            out_shape=jax.ShapeDtypeStruct(panel.shape, panel.dtype),
            in_specs=[
                pl.BlockSpec(memory_space=pltpu.SMEM),
                pl.BlockSpec(memory_space=pl.ANY),
            ],
            out_specs=pl.BlockSpec(memory_space=pl.ANY),
            scratch_shapes=[
                pltpu.VMEM((CHUNKS, chunk, 2 * width), F32),
                pltpu.VMEM((CHUNKS, chunk, width), F32),
                pltpu.VMEM((CHUNKS, chunk, width), F32),
                pltpu.VMEM((STEPS, CHUNKS, chunk, width), F32),
                pltpu.VMEM((STEPS, CHUNKS, chunk, width), F32),
                pltpu.VMEM((2, 2 * width, 2 * width), BF16),
                pltpu.VMEM((STEPS, rows_axis, width, width), F32),
                dma((CHUNKS,)),
                dma((STEPS, max(1, rows_axis - 1))),
                dma((STEPS, max(1, rows_axis - 1))),
                dma((STEPS, CHUNKS)),
                dma((STEPS, CHUNKS)),
                dma((STEPS, CHUNKS)),
                dma((STEPS, CHUNKS)),
                dma((CHUNKS,)),
            ],
            compiler_params=pltpu.CompilerParams(collective_id=0, has_side_effects=True),
        )(slot_block, panel)

    return jax.shard_map(
        per_device,
        mesh=mesh,
        in_specs=(P("row", "pair"), P()),
        out_specs=P("row", "pair"),
        check_vma=False,
    )
```

time: 151 us -> 67.8 us (0.45)
  waiting for transfers between devices: 80.6 us -> 0 us
  Pallas kernels: 0 us -> 64.5 us
  matrix products: 24.9 us -> 0 us
  between operations: 17.7 us -> 0.01 us
  other arithmetic: 12.3 us -> 0 us
  starting transfers between devices: 12.3 us -> 0 us
    pallas_call x0 -> x1, Pallas kernels: none -> 64.5 us  [per_device(): pl.pallas_call(functools.partial(kernel, rows_axis, pairs), out_shape=jax...]
    psum x2 -> x0, waiting for transfers between devices: 43 us -> none  [jacobi_step(): cross = lax.psum(inner_rows(first, second), 'row')]
    ppermute x4 -> x0, waiting for transfers between devices: 37.5 us -> none  [passed_along(): lax.ppermute(value, axis, [(source, source + steps) for source in range(i...]
    dot_general x46 -> x0, matrix products: 24.9 us -> none  [the longest x2 4.89 us: inner_rows(): lax.dot_general(first, second, (((0,), (0,)), ((), ())), precision=precise)]
    ppermute x4 -> x0, starting transfers between devices: 12.2 us -> none  [passed_along(): lax.ppermute(value, axis, [(source, source + steps) for source in range(i...]
    reduce_sum x4 -> x0, other arithmetic: 7.23 us -> none  [the longest x2 3.06 us: couple(): coupling = cross * (2.0 / jnp.sqrt(jnp.sum(cross * cross) + 1e-06))]
    select_n x3 -> x0, other arithmetic: 3.58 us -> none  [the longest x2 3.4 us: jacobi_step(): first = jnp.where(order_flag, upper, lower)]
    unnamed x8 -> x1, local copies, waits for them, and re-layouts: 0.98 us -> 3.05 us
  transfers between devices with their start and end apart: 6 -> 0, of which waited for: 4 -> 0; matrix products, arithmetic and copies ran while one was open for 2% -> 0% of each run, Pallas kernels for 0% -> 0%
where the time goes in v1:
time: 67.8 us; the launch traced here: 67.6 us
  Pallas kernels  64.5 us (95%)
  local copies, waits for them, and re-layouts  3.05 us (4%)
    pallas_call x1, Pallas kernels, per_device(): pl.pallas_call(functools.partial(kernel, rows_axis, pairs), out_shape=jax...  64.5 us
    unnamed x1, local copies, waits for them, and re-layouts  3.05 us

profile of v1, /device:TPU:1, one launch (start us, length us, event | category | flops | bytes accessed | tf_op | source)
XLA Modules:
  0.0 67.6 jit_solution(12056514061654197093)
XLA Ops:
  0.0 64.5 %shard_map.28 = f32[2048,256]{1,0:T(8,128)} custom-call(s32[32]{0:T(128)} %ids.1, f32[2048,256]{1,0:T(8,128)} %panel.1), custom_call_target="tpu_custom_call" | custom-call | tf_op jit(solution)/shard_map/pallas_call | solution.py:286
  64.5 3.0 %copy.4 = f32[2048,256]{1,0:T(8,128)} copy(f32[2048,256]{1,0:T(8,128)} %shard_map.28) | data formatting | bytes 4194304

commit v2 on v1

--- a/solution.py
+++ b/solution.py
@@ -84,13 +84,14 @@
 def kernel(
     rows_axis, pairs, ids, panel, out,
     start, uppers, lowers, to_right, to_left, weights, crosses,
-    load_sem, cross_send, cross_recv, right_send, right_recv, left_send, left_recv, keep_sem,
+    load_sem, cross_send, cross_recv, right_send, right_recv, left_send, left_recv, turn_sem,
 ):
     width = panel.shape[1] // 2
     chunk = panel.shape[0] // CHUNKS
     position = lax.axis_index("pair")
     row = lax.axis_index("row")
     first, last = position == 0, position == pairs - 1
+    odd = lax.rem(position, 2) == 1
     right, left = lax.rem(position + 1, pairs), lax.rem(position + pairs - 1, pairs)
 
     def load(index):
@@ -155,20 +156,6 @@
             device_id_type=MESH,
         )
 
-    def keep_upper(index):
-        return pltpu.make_async_copy(
-            uppers.at[index],
-            out.at[pl.ds(index * chunk, chunk), pl.ds(0, width)],
-            keep_sem.at[index],
-        )
-
-    def keep_lower(index):
-        return pltpu.make_async_copy(
-            lowers.at[index],
-            out.at[pl.ds(index * chunk, chunk), pl.ds(width, width)],
-            keep_sem.at[index],
-        )
-
     def exchange(step, offset):
         peer = lax.rem(row + offset, rows_axis)
         return pltpu.make_async_remote_copy(
@@ -180,6 +167,14 @@
             device_id_type=MESH,
         )
 
+    def start_left(index, carry):
+        send_left(0, index).start()
+        return carry
+
+    def end_right(index, carry):
+        send_right(0, index).wait_send()
+        return carry
+
     for step in range(STEPS):
 
         def halves(index):
@@ -202,7 +197,17 @@
 
             return total + inner_rows(*halves(index))
 
-        total = lax.fori_loop(0, CHUNKS, add_chunk, jnp.zeros((width, width), F32))
+        total = lax.fori_loop(0, CHUNKS - 1, add_chunk, jnp.zeros((width, width), F32))
+        if step == 1:
+            @pl.when(jnp.logical_not(odd))
+            def _():
+                pl.semaphore_wait(turn_sem, 1)
+
+                @pl.when(jnp.logical_not(first))
+                def _():
+                    lax.fori_loop(0, CHUNKS, start_left, 0)
+
+        total = add_chunk(CHUNKS - 1, total)
         crosses[step, row] = total
         if step == 0:
             neighbours = jnp.where(first, 0, 1) + jnp.where(last, 0, 1)
@@ -230,30 +235,48 @@
             def _():
                 send_right(step, index).start()
 
-            @pl.when(jnp.logical_not(first))
+            @pl.when(odd if step == 0 else jnp.logical_not(first))
             def _():
                 send_left(step, index).start()
 
             @pl.when(first)
             def _():
-                uppers[index] = new_upper
                 if step == STEPS - 1:
-                    keep_upper(index).start()
+                    out[pl.ds(index * chunk, chunk), :width] = new_upper
+                else:
+                    uppers[index] = new_upper
 
             @pl.when(last)
             def _():
-                lowers[index] = new_upper
                 if step == STEPS - 1:
-                    keep_lower(index).start()
+                    out[pl.ds(index * chunk, chunk), width:] = new_upper
+                else:
+                    lowers[index] = new_upper
 
             return carry
 
         lax.fori_loop(0, CHUNKS, turn_chunk, 0)
+        if step == 0:
+
+            @pl.when(odd)
+            def _():
+                @pl.when(jnp.logical_not(last))
+                def _():
+                    lax.fori_loop(0, CHUNKS - 1, end_right, 0)
+
+                pl.semaphore_signal(turn_sem, inc=1, device_id={"pair": left}, device_id_type=MESH)
+
+                @pl.when(jnp.logical_not(last))
+                def _():
+                    end_right(CHUNKS - 1, 0)
 
     def finish(index, carry):
         @pl.when(jnp.logical_not(last))
         def _():
-            send_right(0, index).wait_send()
+            @pl.when(jnp.logical_not(odd))
+            def _():
+                send_right(0, index).wait_send()
+
             send_right(1, index).wait_send()
             send_left(1, index).wait_recv()
 
@@ -262,14 +285,6 @@
             send_left(0, index).wait_send()
             send_left(1, index).wait_send()
             send_right(1, index).wait_recv()
-
-        @pl.when(first)
-        def _():
-            keep_upper(index).wait()
-
-        @pl.when(last)
-        def _():
-            keep_lower(index).wait()
 
         return carry
 
@@ -288,9 +303,9 @@
             out_shape=jax.ShapeDtypeStruct(panel.shape, panel.dtype),
             in_specs=[
                 pl.BlockSpec(memory_space=pltpu.SMEM),
-                pl.BlockSpec(memory_space=pl.ANY),
+                pl.BlockSpec(memory_space=pltpu.HBM),
             ],
-            out_specs=pl.BlockSpec(memory_space=pl.ANY),
+            out_specs=pl.BlockSpec(memory_space=pltpu.VMEM),
             scratch_shapes=[
                 pltpu.VMEM((CHUNKS, chunk, 2 * width), F32),
                 pltpu.VMEM((CHUNKS, chunk, width), F32),
@@ -306,9 +321,9 @@
                 dma((STEPS, CHUNKS)),
                 dma((STEPS, CHUNKS)),
                 dma((STEPS, CHUNKS)),
-                dma((CHUNKS,)),
+                pltpu.SemaphoreType.REGULAR,
             ],
-            compiler_params=pltpu.CompilerParams(collective_id=0, has_side_effects=True),
+            compiler_params=pltpu.CompilerParams(collective_id=0, has_side_effects=True, vmem_limit_bytes=10 * panel.size * 4),
         )(slot_block, panel)
 
     return jax.shard_map(

time: 67.8 us -> 61.3 us (0.904)
  Pallas kernels: 64.5 us -> 57.6 us
    pallas_call x1, Pallas kernels: 64.5 us -> 57.6 us  [per_device(): pl.pallas_call(functools.partial(kernel, rows_axis, pairs), out_shape=jax...]
    unnamed x1 -> x5, local copies, waits for them, and re-layouts: 3.05 us -> 3.57 us
where the time goes in v2:
time: 61.3 us; the launch traced here: 61.1 us
  Pallas kernels  57.6 us (94%)
  local copies, waits for them, and re-layouts  3.57 us (6%)
    pallas_call x1, Pallas kernels, per_device(): pl.pallas_call(functools.partial(kernel, rows_axis, pairs), out_shape=jax...  57.6 us
    unnamed x5, local copies, waits for them, and re-layouts  3.57 us

profile of v2, /device:TPU:1, one launch (start us, length us, event | category | flops | bytes accessed | tf_op | source)
XLA Modules:
  0.0 61.1 jit_solution(13651123583755065296)
XLA Ops:
  0.0 0.0 copy-start
  0.0 1.6 %copy-done = f32[2048,256]{1,0:T(8,128)S(1)} copy-done((f32[2048,256]{1,0:T(8,128)S(1)}, f32[2048,256]{1,0:T(8,128)}, u32[]{:S(2)}) %copy-start) | copy-done | bytes 2097176
  1.6 0.0 copy-start.1
  1.6 0.7 %copy-done.1 = s32[32]{0:T(128)S(1)} copy-done((s32[32]{0:T(128)S(1)}, s32[32]{0:T(128)}, u32[]{:S(2)}) %copy-start.1) | copy-done | bytes 152
  2.2 57.6 %shard_map.28 = f32[2048,256]{1,0:T(8,128)S(1)} custom-call(s32[32]{0:T(128)S(1)} %copy-done.1, f32[2048,256]{1,0:T(8,128)S(1)} %copy-done), custom_call_target="tpu_custom_call" | custom-call | tf_op jit(solution)/shard_map/pallas_call | solution.py:301
  59.8 1.3 %copy.4 = f32[2048,256]{1,0:T(8,128)} copy(f32[2048,256]{1,0:T(8,128)S(1)} %shard_map.28) | data formatting | bytes 4194304
Async XLA Ops:
  0.0 1.6 %copy-start = (f32[2048,256]{1,0:T(8,128)S(1)}, f32[2048,256]{1,0:T(8,128)}, u32[]{:S(2)}) copy-start(f32[2048,256]{1,0:T(8,128)} %panel.1) | copy-start | bytes 6291460
  1.6 0.7 %copy-start.1 = (s32[32]{0:T(128)S(1)}, s32[32]{0:T(128)}, u32[]{:S(2)}) copy-start(s32[32]{0:T(128)} %ids.1) | copy-start | bytes 388

commit v3 on v2

--- a/solution.py
+++ b/solution.py
@@ -48,30 +48,30 @@
     return jnp.where(rows == columns, 1.0, 0.0).astype(F32)
 
 
-def inverse_root(matrix, identity):
-    factor = 1.5 * identity - 0.5 * matrix
-    root_inv = factor
-    approx = matrix
-    for sweep in range(1, NS_ITERS):
-        factor_parts = split(factor)
-        approx = product(split(approx), factor_parts)
-        root_parts = split(root_inv)
-        factor = 1.5 * identity - 0.5 * product(root_parts, split(approx))
-        root_inv = product(split(factor), root_parts)
-    return root_inv * (1.0 / math.sqrt(5.0))
-
-
 def rotation(cross, sign):
     identity = identity_of(cross.shape[0])
-    coupling = cross * (sign * (2.0 * lax.rsqrt(jnp.sum(cross * cross, keepdims=True) + 1e-06)))
-    turned = coupling.T
-    coupling_parts, turned_parts = split(coupling), split(turned)
-    left = (identity + product(coupling_parts, turned_parts)) * 0.2
-    right = (identity + product(turned_parts, coupling_parts)) * 0.2
-    left_inverse = inverse_root(left, identity)
-    right_inverse = inverse_root(right, identity)
-    from_lower = product(turned_parts, split(left_inverse))
-    from_upper = -product(coupling_parts, split(right_inverse))
+    scale = 2.0 * lax.rsqrt(jnp.sum(cross * cross, keepdims=True) + 1e-06)
+    turned = cross.T
+    plain_parts, turned_parts = split(cross), split(turned)
+    sides = ((plain_parts, turned_parts), (turned_parts, plain_parts))
+    iterates = [0.2 * identity + (0.2 * scale * scale) * product(a, b) for a, b in sides]
+    factors = [1.5 * identity - 0.5 * value for value in iterates]
+    roots = list(factors)
+    for sweep in range(1, NS_ITERS):
+        parts = [split(value) for value in factors]
+        squares = [product(value, value) for value in parts]
+        iterates = [product(split(a), split(b)) for a, b in zip(iterates, squares)]
+        factors = [1.5 * identity - 0.5 * value for value in iterates]
+        if sweep < NS_ITERS - 1:
+            roots = [product(split(a), split(b)) for a, b in zip(roots, factors)]
+    root_parts = [split(value * (1.0 / math.sqrt(5.0))) for value in roots]
+    mixed = [
+        split((sign * scale) * product(turned_parts, root_parts[0])),
+        split((-sign * scale) * product(plain_parts, root_parts[1])),
+    ]
+    last_parts = [split(value) for value in factors]
+    left_inverse, right_inverse = (product(a, b) for a, b in zip(root_parts, last_parts))
+    from_lower, from_upper = (product(a, b) for a, b in zip(mixed, last_parts))
     return jnp.concatenate(
         [
             jnp.concatenate([left_inverse, from_upper], axis=1),
@@ -84,7 +84,7 @@
 def kernel(
     rows_axis, pairs, ids, panel, out,
     start, uppers, lowers, to_right, to_left, weights, crosses,
-    load_sem, cross_send, cross_recv, right_send, right_recv, left_send, left_recv, turn_sem,
+    load_sem, cross_send, cross_recv, right_send, right_recv, left_send, left_recv, turn_sem, first_sem,
 ):
     width = panel.shape[1] // 2
     chunk = panel.shape[0] // CHUNKS
@@ -213,10 +213,22 @@
             neighbours = jnp.where(first, 0, 1) + jnp.where(last, 0, 1)
             pl.semaphore_wait(barrier, rows_axis - 1 + neighbours)
         copies = [exchange(step, offset) for offset in range(1, rows_axis)]
+        if step == 0:
+
+            @pl.when(jnp.logical_not(odd))
+            def _():
+                pl.semaphore_wait(first_sem, 1)
+
         for copy in copies:
             copy.start()
         for copy in copies:
             copy.wait()
+        if step == 0:
+
+            @pl.when(odd)
+            def _():
+                pl.semaphore_signal(first_sem, inc=1, device_id={"pair": left}, device_id_type=MESH)
+
         cross = crosses[step, 0]
         for index in range(1, rows_axis):
             cross = cross + crosses[step, index]
@@ -300,7 +312,7 @@
         dma = pltpu.SemaphoreType.DMA
         return pl.pallas_call(
             functools.partial(kernel, rows_axis, pairs),
-            out_shape=jax.ShapeDtypeStruct(panel.shape, panel.dtype),
+            out_shape=pltpu.VMEM(panel.shape, panel.dtype),
             in_specs=[
                 pl.BlockSpec(memory_space=pltpu.SMEM),
                 pl.BlockSpec(memory_space=pltpu.HBM),
@@ -322,8 +334,9 @@
                 dma((STEPS, CHUNKS)),
                 dma((STEPS, CHUNKS)),
                 pltpu.SemaphoreType.REGULAR,
+                pltpu.SemaphoreType.REGULAR,
             ],
-            compiler_params=pltpu.CompilerParams(collective_id=0, has_side_effects=True, vmem_limit_bytes=10 * panel.size * 4),
+            compiler_params=pltpu.CompilerParams(collective_id=0, has_side_effects=True, vmem_limit_bytes=67043328 - 3 * panel.size * 4 // 2),
         )(slot_block, panel)
 
     return jax.shard_map(

time: 61.3 us -> 59.2 us (0.966)
  local copies, waits for them, and re-layouts: 3.57 us -> 1.32 us
    unnamed x5 -> x1, local copies, waits for them, and re-layouts: 3.57 us -> 1.32 us
where the time goes in v3:
time: 59.2 us; the launch traced here: 59 us
  Pallas kernels  57.7 us (97%)
  local copies, waits for them, and re-layouts  1.32 us (2%)
    pallas_call x1, Pallas kernels, per_device(): pl.pallas_call(functools.partial(kernel, rows_axis, pairs), out_shape=plt...  57.7 us
    unnamed x1, local copies, waits for them, and re-layouts  1.32 us

profile of v3, /device:TPU:1, one launch (start us, length us, event | category | flops | bytes accessed | tf_op | source)
XLA Modules:
  0.0 59.0 jit_solution(3313068232976428386)
XLA Ops:
  0.0 57.7 %shard_map.28 = f32[2048,256]{1,0:T(8,128)S(1)} custom-call(s32[32]{0:T(128)} %ids.1, f32[2048,256]{1,0:T(8,128)} %panel.1), custom_call_target="tpu_custom_call" | custom-call | tf_op jit(solution)/shard_map/pallas_call | solution.py:313
  57.7 1.3 %copy.4 = f32[2048,256]{1,0:T(8,128)} copy(f32[2048,256]{1,0:T(8,128)S(1)} %shard_map.28) | data formatting | bytes 4194304

commit v4 on v3

--- a/solution.py
+++ b/solution.py
@@ -11,6 +11,7 @@
 STEPS = 2
 NS_ITERS = 3
 CHUNKS = 8
+RAW = 2
 MESH = pl.DeviceIdType.MESH
 F32 = jnp.float32
 BF16 = jnp.bfloat16
@@ -83,8 +84,8 @@
 
 def kernel(
     rows_axis, pairs, ids, panel, out,
-    start, uppers, lowers, to_right, to_left, weights, crosses,
-    load_sem, cross_send, cross_recv, right_send, right_recv, left_send, left_recv, turn_sem, first_sem,
+    start, uppers, lowers, raw, mine, theirs, their_weights, to_right, to_left, weights, crosses,
+    load_sem, cross_send, cross_recv, right_send, right_recv, left_send, left_recv, raw_send, raw_recv, turn_sem, first_sem,
 ):
     width = panel.shape[1] // 2
     chunk = panel.shape[0] // CHUNKS
@@ -92,6 +93,9 @@
     row = lax.axis_index("row")
     first, last = position == 0, position == pairs - 1
     odd = lax.rem(position, 2) == 1
+    even = jnp.logical_not(odd)
+    sends_raw = jnp.logical_and(odd, jnp.logical_not(last))
+    takes_raw = jnp.logical_and(even, jnp.logical_not(first))
     right, left = lax.rem(position + 1, pairs), lax.rem(position + pairs - 1, pairs)
 
     def load(index):
@@ -117,6 +121,36 @@
     @pl.when(jnp.logical_not(last))
     def _():
         pl.semaphore_signal(barrier, inc=1, device_id={"pair": right}, device_id_type=MESH)
+
+    neighbours = jnp.where(first, 0, 1) + jnp.where(last, 0, 1)
+    pl.semaphore_wait(barrier, rows_axis - 1 + neighbours)
+
+    def send_raw(index):
+        return pltpu.make_async_remote_copy(
+            src_ref=start.at[index],
+            dst_ref=raw.at[index],
+            send_sem=raw_send.at[index],
+            recv_sem=raw_recv.at[index],
+            device_id={"pair": right},
+            device_id_type=MESH,
+        )
+
+    def send_cross():
+        return pltpu.make_async_remote_copy(
+            src_ref=mine,
+            dst_ref=theirs,
+            send_sem=raw_send.at[RAW],
+            recv_sem=raw_recv.at[RAW],
+            device_id={"pair": right},
+            device_id_type=MESH,
+        )
+
+    for index in range(RAW):
+        load(index).wait()
+
+        @pl.when(sends_raw)
+        def _():
+            send_raw(index).start()
 
     def sign_of(upper_id, lower_id):
         return jnp.where(upper_id < lower_id, 1.0, -1.0).astype(F32)
@@ -127,6 +161,7 @@
         sign_of(ids[position], ids[pairs + position]),
         sign_of(moved_upper, moved_lower),
     )
+    left_sign = sign_of(ids[left], ids[pairs + left])
 
     def send_right(step, index):
         if step == 0:
@@ -184,10 +219,14 @@
 
         def add_chunk(index, total):
             if step == 0:
-                load(index).wait()
+
+                @pl.when(index >= RAW)
+                def _():
+                    load(index).wait()
+
             else:
 
-                @pl.when(jnp.logical_not(first))
+                @pl.when(jnp.logical_and(jnp.logical_not(first), jnp.logical_or(odd, index >= RAW)))
                 def _():
                     send_right(0, index).wait_recv()
 
@@ -209,9 +248,6 @@
 
         total = add_chunk(CHUNKS - 1, total)
         crosses[step, row] = total
-        if step == 0:
-            neighbours = jnp.where(first, 0, 1) + jnp.where(last, 0, 1)
-            pl.semaphore_wait(barrier, rows_axis - 1 + neighbours)
         copies = [exchange(step, offset) for offset in range(1, rows_axis)]
         if step == 0:
 
@@ -232,10 +268,18 @@
         cross = crosses[step, 0]
         for index in range(1, rows_axis):
             cross = cross + crosses[step, index]
+        if step == 0:
+
+            @pl.when(sends_raw)
+            def _():
+                mine[...] = cross
+                send_cross().start()
+
         for part, value in enumerate(split(rotation(cross, signs[step]))):
             weights[part] = value
 
-        def turn_chunk(index, carry):
+        def turn_chunk(turn, carry):
+            index = lax.rem(turn + RAW, CHUNKS) if step == 0 else turn
             upper, lower = halves(index)
             parts = split(jnp.concatenate([upper, lower], axis=1))
             turned = product(parts, (weights[0], weights[1]))
@@ -243,7 +287,11 @@
             to_right[step, index] = jnp.where(first, new_lower, new_upper)
             to_left[step, index] = new_lower
 
-            @pl.when(jnp.logical_not(last))
+            sends = jnp.logical_not(last)
+            if step == 0:
+                sends = jnp.logical_and(sends, jnp.logical_or(even, index >= RAW))
+
+            @pl.when(sends)
             def _():
                 send_right(step, index).start()
 
@@ -274,13 +322,25 @@
             def _():
                 @pl.when(jnp.logical_not(last))
                 def _():
-                    lax.fori_loop(0, CHUNKS - 1, end_right, 0)
+                    lax.fori_loop(RAW, CHUNKS - 1, end_right, 0)
 
                 pl.semaphore_signal(turn_sem, inc=1, device_id={"pair": left}, device_id_type=MESH)
 
                 @pl.when(jnp.logical_not(last))
                 def _():
                     end_right(CHUNKS - 1, 0)
+                    send_cross().wait_send()
+                    for index in range(RAW):
+                        send_raw(index).wait_send()
+
+            @pl.when(takes_raw)
+            def _():
+                send_cross().wait_recv()
+                for part, value in enumerate(split(rotation(theirs[...], left_sign)[:, :width])):
+                    their_weights[part] = value
+                for index in range(RAW):
+                    send_raw(index).wait_recv()
+                    uppers[index] = product(split(raw[index]), (their_weights[0], their_weights[1]))
 
     def finish(index, carry):
         @pl.when(jnp.logical_not(last))
@@ -322,6 +382,10 @@
                 pltpu.VMEM((CHUNKS, chunk, 2 * width), F32),
                 pltpu.VMEM((CHUNKS, chunk, width), F32),
                 pltpu.VMEM((CHUNKS, chunk, width), F32),
+                pltpu.VMEM((RAW, chunk, 2 * width), F32),
+                pltpu.VMEM((width, width), F32),
+                pltpu.VMEM((width, width), F32),
+                pltpu.VMEM((2, 2 * width, width), BF16),
                 pltpu.VMEM((STEPS, CHUNKS, chunk, width), F32),
                 pltpu.VMEM((STEPS, CHUNKS, chunk, width), F32),
                 pltpu.VMEM((2, 2 * width, 2 * width), BF16),
@@ -333,6 +397,8 @@
                 dma((STEPS, CHUNKS)),
                 dma((STEPS, CHUNKS)),
                 dma((STEPS, CHUNKS)),
+                dma((RAW + 1,)),
+                dma((RAW + 1,)),
                 pltpu.SemaphoreType.REGULAR,
                 pltpu.SemaphoreType.REGULAR,
             ],

time: 59.2 us -> 57.7 us (0.975)
  Pallas kernels: 57.7 us -> 56.2 us
    pallas_call x1, Pallas kernels: 57.7 us -> 56.2 us  [per_device(): pl.pallas_call(functools.partial(kernel, rows_axis, pairs), out_shape=plt...]
where the time goes in v4:
time: 57.7 us; the launch traced here: 57.5 us
  Pallas kernels  56.2 us (97%)
  local copies, waits for them, and re-layouts  1.32 us (2%)
    pallas_call x1, Pallas kernels, per_device(): pl.pallas_call(functools.partial(kernel, rows_axis, pairs), out_shape=plt...  56.2 us
    unnamed x1, local copies, waits for them, and re-layouts  1.32 us

profile of v4, /device:TPU:1, one launch (start us, length us, event | category | flops | bytes accessed | tf_op | source)
XLA Modules:
  0.0 57.5 jit_solution(6203787808272085874)
XLA Ops:
  0.0 56.2 %shard_map.28 = f32[2048,256]{1,0:T(8,128)S(1)} custom-call(s32[32]{0:T(128)} %ids.1, f32[2048,256]{1,0:T(8,128)} %panel.1), custom_call_target="tpu_custom_call" | custom-call | tf_op jit(solution)/shard_map/pallas_call | solution.py:373
  56.2 1.3 %copy.4 = f32[2048,256]{1,0:T(8,128)} copy(f32[2048,256]{1,0:T(8,128)S(1)} %shard_map.28) | data formatting | bytes 4194304

commit v5 on v4

--- a/solution.py
+++ b/solution.py
@@ -123,7 +123,6 @@
         pl.semaphore_signal(barrier, inc=1, device_id={"pair": right}, device_id_type=MESH)
 
     neighbours = jnp.where(first, 0, 1) + jnp.where(last, 0, 1)
-    pl.semaphore_wait(barrier, rows_axis - 1 + neighbours)
 
     def send_raw(index):
         return pltpu.make_async_remote_copy(
@@ -144,13 +143,6 @@
             device_id={"pair": right},
             device_id_type=MESH,
         )
-
-    for index in range(RAW):
-        load(index).wait()
-
-        @pl.when(sends_raw)
-        def _():
-            send_raw(index).start()
 
     def sign_of(upper_id, lower_id):
         return jnp.where(upper_id < lower_id, 1.0, -1.0).astype(F32)
@@ -217,36 +209,43 @@
                 return start[index, :, :width], start[index, :, width:]
             return uppers[index], lowers[index]
 
-        def add_chunk(index, total):
+        def await_chunk(index):
             if step == 0:
-
-                @pl.when(index >= RAW)
+                load(index).wait()
+                return
+
+            @pl.when(jnp.logical_not(first) if index >= RAW else jnp.logical_and(odd, jnp.logical_not(first)))
+            def _():
+                send_right(0, index).wait_recv()
+
+            @pl.when(jnp.logical_not(last))
+            def _():
+                send_left(0, index).wait_recv()
+
+        group = CHUNKS // 2 if step == 0 else CHUNKS // 4
+        total = jnp.zeros((width, width), F32)
+        for lead in range(0, CHUNKS, group):
+            if step == 1 and lead == CHUNKS - group:
+                @pl.when(even)
                 def _():
-                    load(index).wait()
-
-            else:
-
-                @pl.when(jnp.logical_and(jnp.logical_not(first), jnp.logical_or(odd, index >= RAW)))
+                    pl.semaphore_wait(turn_sem, 1)
+
+                    @pl.when(jnp.logical_not(first))
+                    def _():
+                        lax.fori_loop(0, CHUNKS, start_left, 0)
+
+            for index in range(lead, lead + group):
+                await_chunk(index)
+            for index in range(lead, lead + group):
+                total = total + inner_rows(*halves(index))
+            if step == 0 and lead == 0:
+                pl.semaphore_wait(barrier, rows_axis - 1 + neighbours)
+
+                @pl.when(sends_raw)
                 def _():
-                    send_right(0, index).wait_recv()
-
-                @pl.when(jnp.logical_not(last))
-                def _():
-                    send_left(0, index).wait_recv()
-
-            return total + inner_rows(*halves(index))
-
-        total = lax.fori_loop(0, CHUNKS - 1, add_chunk, jnp.zeros((width, width), F32))
-        if step == 1:
-            @pl.when(jnp.logical_not(odd))
-            def _():
-                pl.semaphore_wait(turn_sem, 1)
-
-                @pl.when(jnp.logical_not(first))
-                def _():
-                    lax.fori_loop(0, CHUNKS, start_left, 0)
-
-        total = add_chunk(CHUNKS - 1, total)
+                    for index in range(RAW):
+                        send_raw(index).start()
+
         crosses[step, row] = total
         copies = [exchange(step, offset) for offset in range(1, rows_axis)]
         if step == 0:
@@ -322,12 +321,13 @@
             def _():
                 @pl.when(jnp.logical_not(last))
                 def _():
-                    lax.fori_loop(RAW, CHUNKS - 1, end_right, 0)
+                    lax.fori_loop(RAW, CHUNKS - 2, end_right, 0)
 
                 pl.semaphore_signal(turn_sem, inc=1, device_id={"pair": left}, device_id_type=MESH)
 
                 @pl.when(jnp.logical_not(last))
                 def _():
+                    end_right(CHUNKS - 2, 0)
                     end_right(CHUNKS - 1, 0)
                     send_cross().wait_send()
                     for index in range(RAW):

time: 57.7 us -> 56 us (0.971)
  Pallas kernels: 56.2 us -> 54.5 us
    pallas_call x1, Pallas kernels: 56.2 us -> 54.5 us  [per_device(): pl.pallas_call(functools.partial(kernel, rows_axis, pairs), out_shape=plt...]
where the time goes in v5:
time: 56 us; the launch traced here: 55.8 us
  Pallas kernels  54.5 us (97%)
  local copies, waits for them, and re-layouts  1.32 us (2%)
    pallas_call x1, Pallas kernels, per_device(): pl.pallas_call(functools.partial(kernel, rows_axis, pairs), out_shape=plt...  54.5 us
    unnamed x1, local copies, waits for them, and re-layouts  1.32 us

profile of v5, /device:TPU:1, one launch (start us, length us, event | category | flops | bytes accessed | tf_op | source)
XLA Modules:
  0.0 55.8 jit_solution(7265094274227200518)
XLA Ops:
  0.0 54.5 %shard_map.28 = f32[2048,256]{1,0:T(8,128)S(1)} custom-call(s32[32]{0:T(128)} %ids.1, f32[2048,256]{1,0:T(8,128)} %panel.1), custom_call_target="tpu_custom_call" | custom-call | tf_op jit(solution)/shard_map/pallas_call | solution.py:373
  54.5 1.3 %copy.4 = f32[2048,256]{1,0:T(8,128)} copy(f32[2048,256]{1,0:T(8,128)S(1)} %shard_map.28) | data formatting | bytes 4194304

commit v6 on v5

--- a/solution.py
+++ b/solution.py
@@ -10,8 +10,8 @@
 
 STEPS = 2
 NS_ITERS = 3
-CHUNKS = 8
-RAW = 2
+CHUNKS = 4
+RAW = 1
 MESH = pl.DeviceIdType.MESH
 F32 = jnp.float32
 BF16 = jnp.bfloat16
@@ -84,7 +84,7 @@
 
 def kernel(
     rows_axis, pairs, ids, panel, out,
-    start, uppers, lowers, raw, mine, theirs, their_weights, to_right, to_left, weights, crosses,
+    start, uppers, lowers, raw, mine, theirs, their_weights, to_right, to_left, landed, weights, crosses,
     load_sem, cross_send, cross_recv, right_send, right_recv, left_send, left_recv, raw_send, raw_recv, turn_sem, first_sem,
 ):
     width = panel.shape[1] // 2
@@ -159,7 +159,7 @@
         if step == 0:
             target = uppers.at[index]
         else:
-            target = out.at[pl.ds(index * chunk, chunk), pl.ds(0, width)]
+            target = landed.at[0, index]
         return pltpu.make_async_remote_copy(
             src_ref=to_right.at[step, index],
             dst_ref=target,
@@ -173,7 +173,7 @@
         if step == 0:
             target = lowers.at[index]
         else:
-            target = out.at[pl.ds(index * chunk, chunk), pl.ds(width, width)]
+            target = landed.at[1, index]
         return pltpu.make_async_remote_copy(
             src_ref=to_left.at[step, index],
             dst_ref=target,
@@ -321,14 +321,13 @@
             def _():
                 @pl.when(jnp.logical_not(last))
                 def _():
-                    lax.fori_loop(RAW, CHUNKS - 2, end_right, 0)
+                    lax.fori_loop(RAW, CHUNKS - CHUNKS // 4, end_right, 0)
 
                 pl.semaphore_signal(turn_sem, inc=1, device_id={"pair": left}, device_id_type=MESH)
 
                 @pl.when(jnp.logical_not(last))
                 def _():
-                    end_right(CHUNKS - 2, 0)
-                    end_right(CHUNKS - 1, 0)
+                    lax.fori_loop(CHUNKS - CHUNKS // 4, CHUNKS, end_right, 0)
                     send_cross().wait_send()
                     for index in range(RAW):
                         send_raw(index).wait_send()
@@ -351,12 +350,14 @@
 
             send_right(1, index).wait_send()
             send_left(1, index).wait_recv()
+            out[pl.ds(index * chunk, chunk), width:] = landed[1, index]
 
         @pl.when(jnp.logical_not(first))
         def _():
             send_left(0, index).wait_send()
             send_left(1, index).wait_send()
             send_right(1, index).wait_recv()
+            out[pl.ds(index * chunk, chunk), :width] = landed[0, index]
 
         return carry
 
@@ -388,6 +389,7 @@
                 pltpu.VMEM((2, 2 * width, width), BF16),
                 pltpu.VMEM((STEPS, CHUNKS, chunk, width), F32),
                 pltpu.VMEM((STEPS, CHUNKS, chunk, width), F32),
+                pltpu.VMEM((2, CHUNKS, chunk, width), F32),
                 pltpu.VMEM((2, 2 * width, 2 * width), BF16),
                 pltpu.VMEM((STEPS, rows_axis, width, width), F32),
                 dma((CHUNKS,)),

time: 56 us -> 55.7 us (level)
  no operation moved by 1% of the time
where the time goes in v6:
time: 55.7 us; the launch traced here: 55.5 us
  Pallas kernels  54.2 us (97%)
  local copies, waits for them, and re-layouts  1.32 us (2%)
    pallas_call x1, Pallas kernels, per_device(): pl.pallas_call(functools.partial(kernel, rows_axis, pairs), out_shape=plt...  54.2 us
    unnamed x1, local copies, waits for them, and re-layouts  1.32 us

profile of v6, /device:TPU:1, one launch (start us, length us, event | category | flops | bytes accessed | tf_op | source)
XLA Modules:
  0.0 55.5 jit_solution(17338066443665199907)
XLA Ops:
  0.0 54.2 %shard_map.28 = f32[2048,256]{1,0:T(8,128)S(1)} custom-call(s32[32]{0:T(128)} %ids.1, f32[2048,256]{1,0:T(8,128)} %panel.1), custom_call_target="tpu_custom_call" | custom-call | tf_op jit(solution)/shard_map/pallas_call | solution.py:374
  54.2 1.3 %copy.4 = f32[2048,256]{1,0:T(8,128)} copy(f32[2048,256]{1,0:T(8,128)S(1)} %shard_map.28) | data formatting | bytes 4194304
